TPU v7x, 512 devices: a whole 4x4x16 slice. The times are simulated.
512 devices in a mesh: dp: 64 (over y, z), mp: 8 (over x, core).
Axes of the slice: x: 4, y: 4, z: 16, core: 2. Of those that a mesh axis runs over, the one named last changes fastest.
Arguments:
- x_in: bfloat16 [25600, 2048], P('dp'), may hold values from -6 to 6
- cotangent: bfloat16 [25600, 7168], P('dp', 'mp'), may hold values from -6 to 6
- w_gate: bfloat16 [2048, 7168], P('dp', 'mp'), may hold values from -0.125 to 0.125
- w_up: bfloat16 [2048, 7168], P('dp', 'mp'), may hold values from -0.125 to 0.125
- send_counts: int32 [64, 64], P('dp'), may hold values from 0 to 4, as said below
- recv_counts: int32 [64, 64], P('dp'), may hold values from 0 to 4, as said below
Outputs:
- grad_x: bfloat16 [25600, 2048], P('dp', 'mp')
- grad_gate: float32 [2048, 7168], P('dp', 'mp')
Inputs may be any that keep to these rules, and one draw needn't show every extreme that they name: `send_counts`: each entry is 0 to 4. A quarter of the indices only send and the rest only receive; one sending index sends 4 rows to every receiver, so its live rows reach 400. recv_counts is the transpose of send_counts.
All inputs are finite; a program needn't handle non-finite values.
Results may differ from a plain program's by a relative error of at most 0.014.
Values may be sent and summed in bfloat16 or wider, within the bound.
A program may use at most 64 MiB of HBM per device.

v0:
```python
import jax
import jax.numpy as jnp
from jax import lax
from jax.sharding import PartitionSpec as P

BAL = 208


def contract_last(left, right):
    return lax.dot_general(
        left, right, (((1,), (1,)), ((), ())), preferred_element_type=jnp.float32
    )


def swiglu_back(x_rows, cot_rows, gate_full, up_full, live_mask):
    gate_val = jnp.dot(x_rows, gate_full, preferred_element_type=jnp.float32)
    up_val = jnp.dot(x_rows, up_full, preferred_element_type=jnp.float32)
    sig = jax.nn.sigmoid(gate_val)
    cot_val = cot_rows.astype(jnp.float32)
    d_gate = jnp.where(
        live_mask[:, None], cot_val * up_val * sig * (1.0 + gate_val * (1.0 - sig)), 0.0
    ).astype(jnp.bfloat16)
    d_up = jnp.where(live_mask[:, None], cot_val * gate_val * sig, 0.0).astype(jnp.bfloat16)
    partial_value = contract_last(d_gate, gate_full) + contract_last(d_up, up_full)
    return (partial_value, d_gate)


def group_sum(partial_value):
    return lax.psum_scatter(
        partial_value.astype(jnp.bfloat16), "mp", scatter_dimension=1, tiled=True
    )


def on_device(x_in, cotangent, w_gate, w_up, send_counts, recv_counts):
    rows_cap = x_in.shape[0]
    width = x_in.shape[1]
    dev_count = lax.axis_size("dp")
    gate_full, up_full = (
        lax.all_gather(w_gate, "dp", axis=0, tiled=True),
        lax.all_gather(w_up, "dp", axis=0, tiled=True),
    )
    sent = send_counts[0]
    got = recv_counts[0]
    live_rows = BAL + jnp.sum(sent) - jnp.sum(got)
    live_mask = jnp.arange(rows_cap) < live_rows
    partial_value, d_gate = swiglu_back(x_in, cotangent, gate_full, up_full, live_mask)
    grad_x = group_sum(partial_value)
    block_rows = width // dev_count
    whole = lax.dot_general(
        x_in, d_gate, (((0,), (0,)), ((), ())), preferred_element_type=jnp.float32
    )
    grad_gate = lax.psum_scatter(
        whole.astype(jnp.bfloat16), "dp", scatter_dimension=0, tiled=True
    ).astype(jnp.float32)
    return (grad_x, grad_gate)


def solution(mesh):
    return jax.shard_map(
        on_device,
        mesh=mesh,
        in_specs=(
            P("dp", None),
            P("dp", "mp"),
            P("dp", "mp"),
            P("dp", "mp"),
            P("dp", None),
            P("dp", None),
        ),
        out_specs=(P("dp", "mp"), P("dp", "mp")),
        check_vma=False,
    )
```

profile of v0, /device:TPU:8, one launch (start us, length us, event | category | flops | bytes accessed | tf_op | source)
XLA Modules:
  0.0 1060.5 jit_solution(8219626550588682840)
XLA Ops:
  7.2 0.0 copy-start
  7.2 0.0 all-gather.5.cloned.1.call-start
  7.2 0.7 all-gather.5.cloned.1.call-update
  7.9 0.0 all-gather.3.cloned.1.call-start
  8.0 0.7 all-gather.3.cloned.1.call-update
  8.7 0.0 reduce-scatter.7.cloned.1.call-start
  8.7 1.3 reduce_sum.19
  10.0 1.3 reduce_sum.18
  12.6 0.0 copy-start.2
  12.6 147.1 %all-gather.5.cloned.1.call-done = bf16[2048,896]{1,0:T(8,128)(2,1)} async-done(((bf16[32,896]{1,0:T(8,128)(2,1)}), bf16[2048,896]{1,0:T(8,128)(2,1)}) %all-gather.5.cloned.1.call-update) | async-done | bytes 3670032 | tf_op jit(solution)/shard_map/all_gather | solution.py:39
  159.7 0.0 copy-done
  159.7 5.0 fusion.11
  164.7 137.7 %all-gather.3.cloned.1.call-done = bf16[2048,896]{1,0:T(8,128)(2,1)} async-done(((bf16[32,896]{1,0:T(8,128)(2,1)}), bf16[2048,896]{1,0:T(8,128)(2,1)}) %all-gather.3.cloned.1.call-update) | async-done | bytes 3670032 | tf_op jit(solution)/shard_map/all_gather | solution.py:40
  302.4 0.0 copy-done.2
  302.4 4.6 select_convert_fusion
  307.0 4.0 convert_bitcast_fusion
  311.0 6.1 copy.10
  317.1 0.0 reduce-scatter.7.cloned.1.call-update
  317.2 0.0 reduce-scatter.5.cloned.1.call-start
  317.2 0.0 copy-start.1
  317.2 0.0 copy-start.3
  317.2 4.1 fusion.12
  321.3 0.0 copy-done.1
  321.3 0.0 copy-done.3
  321.3 3.1 add_convert_fusion
  324.5 0.0 reduce-scatter.5.cloned.1.call-update
  324.5 687.3 %reduce-scatter.7.cloned.1.call-done = bf16[32,896]{1,0:T(8,128)(2,1)} async-done(((bf16[2048,896]{1,0:T(8,128)(2,1)}), bf16[32,896]{1,0:T(8,128)(2,1)}) %reduce-scatter.7.cloned.1.call-update) | async-done | bytes 57360
  1011.7 1.0 copy.11
  1012.7 0.8 copy.9
  1013.5 40.4 %reduce-scatter.5.cloned.1.call-done = bf16[400,256]{1,0:T(8,128)(2,1)} async-done(((bf16[400,2048]{1,0:T(8,128)(2,1)}), bf16[400,256]{1,0:T(8,128)(2,1)}) %reduce-scatter.5.cloned.1.call-update) | async-done | bytes 204816 | tf_op jit(solution)/shard_map/reduce_scatter | solution.py:29
  (1 shorter events, 0.0 us)
Async XLA Ops:
  7.2 152.6 %copy-start = (bf16[400,2048]{1,0:T(8,128)(2,1)S(1)}, bf16[400,2048]{1,0:T(8,128)(2,1)}, u32[]{:S(2)}) copy-start(bf16[400,2048]{1,0:T(8,128)(2,1)} %param.6) | copy-start | bytes 4915204
  7.2 152.5 %all-gather.5.cloned.1.call-start = ((), (), s32[]{:S(2)}) async-start(), calls=%async_computation.3 | async-start | bytes 3727360 | tf_op jit(solution)/shard_map/all_gather | solution.py:39
  7.9 294.5 %all-gather.3.cloned.1.call-start = ((), (), s32[]{:S(2)}) async-start(), calls=%async_computation.2 | async-start | bytes 3727360 | tf_op jit(solution)/shard_map/all_gather | solution.py:40
  8.7 1003.1 %reduce-scatter.7.cloned.1.call-start = ((), (), s32[]{:S(2)}) async-start(), calls=%async_computation.5 | async-start | bytes 3727360
  12.6 289.8 %copy-start.2 = (bf16[400,896]{1,0:T(8,128)(2,1)S(1)}, bf16[400,896]{1,0:T(8,128)(2,1)}, u32[]{:S(2)}) copy-start(bf16[400,896]{1,0:T(8,128)(2,1)} %param.7) | copy-start | bytes 2150404
  317.2 736.8 %reduce-scatter.5.cloned.1.call-start = ((), (), s32[]{:S(2)}) async-start(), calls=%async_computation.4 | async-start | bytes 1843200 | tf_op jit(solution)/shard_map/reduce_scatter | solution.py:29
  317.2 4.1 copy-start.1
  317.2 4.1 copy-start.3
Sparse Core Ops, SparseCore 0:
  11.0 148.7 all-gather.4
  162.7 139.7 all-gather.2
  317.3 694.4 reduce-scatter.6
  1015.3 38.6 reduce-scatter.4
where the time goes:
time: 1060 us
  waiting for transfers between devices  1010 us (95%)
  matrix products  20.8 us (2%)
  between operations  15.1 us (1%)
    unnamed x5, waiting for transfers between devices  689 us
    all_gather x1, waiting for transfers between devices, on_device(): lax.all_gather(w_gate, 'dp', axis=0, tiled=True)  147 us
    all_gather x1, waiting for transfers between devices, on_device(): lax.all_gather(w_up, 'dp', axis=0, tiled=True)  138 us
    reduce_scatter x1, waiting for transfers between devices, group_sum(): lax.psum_scatter(partial_value.astype(jnp.bfloat16), 'mp', scatter_dimens...  40.4 us
  transfers between devices with their start and end apart: 4, of which 4 were waited for; matrix products, arithmetic and copies ran while one was open for 2% of the time, Pallas kernels for 0%

commit v1 on v0

--- a/solution.py
+++ b/solution.py
@@ -1,9 +1,23 @@
+import functools
 import jax
 import jax.numpy as jnp
 from jax import lax
 from jax.sharding import PartitionSpec as P
 
 BAL = 208
+
+
+def serve_column(z_in, axis_name, dimension_no):
+    return lax.all_to_all(
+        jnp.concatenate([z_in] * lax.psum(1, axis_name), dimension_no),
+        axis_name,
+        dimension_no,
+        dimension_no,
+        tiled=True,
+    )
+
+
+columns_compute = functools.partial(serve_column, axis_name="dp", dimension_no=0)
 
 
 def contract_last(left, right):
@@ -35,10 +49,7 @@
     rows_cap = x_in.shape[0]
     width = x_in.shape[1]
     dev_count = lax.axis_size("dp")
-    gate_full, up_full = (
-        lax.all_gather(w_gate, "dp", axis=0, tiled=True),
-        lax.all_gather(w_up, "dp", axis=0, tiled=True),
-    )
+    gate_full, up_full = (lax.all_gather(w_gate, "dp", axis=0, tiled=True), columns_compute(w_up))
     sent = send_counts[0]
     got = recv_counts[0]
     live_rows = BAL + jnp.sum(sent) - jnp.sum(got)

time: 1060 us -> 1020 us (0.962)
  waiting for transfers between devices: 1010 us -> 925 us
  local copies, waits for them, and re-layouts: 7.91 us -> 36.9 us
  starting transfers between devices: 0.16 us -> 19.2 us
    all_gather x1 -> x0, waiting for transfers between devices: 138 us -> none  [on_device(): lax.all_gather(w_up, 'dp', axis=0, tiled=True)]
    all_gather x1, waiting for transfers between devices: 147 us -> 198 us  [on_device(): lax.all_gather(w_gate, 'dp', axis=0, tiled=True)]
    unnamed x11 -> x80, local copies, waits for them, and re-layouts: 7.91 us -> 36.9 us
    all_to_all x0 -> x1, starting transfers between devices: none -> 19 us  [serve_column(): lax.all_to_all(jnp.concatenate([z_in] * lax.psum(1, axis_name), dimension...]
    unnamed x5 -> x4, waiting for transfers between devices: 689 us -> 687 us
  transfers between devices with their start and end apart: 4 -> 4, of which waited for: 4 -> 3; matrix products, arithmetic and copies ran while one was open for 2% -> 2% of each run, Pallas kernels for 0% -> 0%
where the time goes in v1:
time: 1020 us
  waiting for transfers between devices  925 us (91%)
  local copies, waits for them, and re-layouts  36.9 us (4%)
  matrix products  22.8 us (2%)
  starting transfers between devices  19.2 us (2%)
  between operations  15.3 us (2%)
    unnamed x4, waiting for transfers between devices  687 us
    all_gather x1, waiting for transfers between devices, on_device(): lax.all_gather(w_gate, 'dp', axis=0, tiled=True)  198 us
    reduce_scatter x1, waiting for transfers between devices, group_sum(): lax.psum_scatter(partial_value.astype(jnp.bfloat16), 'mp', scatter_dimens...  40.5 us
    unnamed x80, local copies, waits for them, and re-layouts  36.9 us
  transfers between devices with their start and end apart: 4, of which 3 were waited for; matrix products, arithmetic and copies ran while one was open for 2% of the time, Pallas kernels for 0%

profile of v1, /device:TPU:8, one launch (start us, length us, event | category | flops | bytes accessed | tf_op | source)
XLA Modules:
  0.0 1020.2 jit_solution(2516748521423423073)
XLA Ops:
  7.2 1.0 constant_dynamic-update-slice_fusion.63
  8.2 0.8 constant_dynamic-update-slice_fusion.62
  9.0 0.8 constant_dynamic-update-slice_fusion.61
  9.8 0.8 constant_dynamic-update-slice_fusion.60
  10.6 0.8 constant_dynamic-update-slice_fusion.59
  11.5 0.8 constant_dynamic-update-slice_fusion.58
  12.3 0.8 constant_dynamic-update-slice_fusion.57
  13.1 0.8 constant_dynamic-update-slice_fusion.56
  14.0 0.8 constant_dynamic-update-slice_fusion.55
  14.8 0.8 constant_dynamic-update-slice_fusion.54
  15.6 0.8 constant_dynamic-update-slice_fusion.53
  16.5 0.8 constant_dynamic-update-slice_fusion.52
  17.3 0.8 constant_dynamic-update-slice_fusion.51
  18.1 0.8 constant_dynamic-update-slice_fusion.50
  18.9 0.8 constant_dynamic-update-slice_fusion.49
  19.8 0.8 constant_dynamic-update-slice_fusion.48
  20.6 0.8 constant_dynamic-update-slice_fusion.47
  21.4 0.8 constant_dynamic-update-slice_fusion.46
  22.3 0.8 constant_dynamic-update-slice_fusion.45
  23.1 0.8 constant_dynamic-update-slice_fusion.44
  34.4 1.9 copy-done.2
  36.4 19.0 %all-to-all-start = ((bf16[64,32,896]{2,1,0:T(8,128)(2,1)}), bf16[64,32,896]{2,1,0:T(8,128)(2,1)}, u32[]{:S(2)}, u32[]{:S(2)}) async-start(bf16[64,32,896]{2,1,0:T(8,128)(2,1)} %bitcast.24), calls=%async_computation | async-start | bytes 7340032 | tf_op jit(solution)/shard_map/all_to_all | solution.py:11
  58.8 197.7 %all-gather.2.cloned.1.call-done = bf16[2048,896]{1,0:T(8,128)(2,1)} async-done(((bf16[32,896]{1,0:T(8,128)(2,1)}), bf16[2048,896]{1,0:T(8,128)(2,1)}) %all-gather.2.cloned.1.call-update) | async-done | bytes 3670032 | tf_op jit(solution)/shard_map/all_gather | solution.py:52
  256.5 5.0 fusion.11
  261.5 4.6 select_convert_fusion
  266.1 4.0 convert_bitcast_fusion
  270.1 6.1 copy.10
  276.3 4.0 fusion.12
  280.4 5.1 add_convert_fusion
  285.6 685.9 %reduce-scatter.7.cloned.1.call-done = bf16[32,896]{1,0:T(8,128)(2,1)} async-done(((bf16[2048,896]{1,0:T(8,128)(2,1)}), bf16[32,896]{1,0:T(8,128)(2,1)}) %reduce-scatter.7.cloned.1.call-update) | async-done | bytes 57360
  971.5 1.0 copy.11
  973.2 40.5 %reduce-scatter.5.cloned.1.call-done = bf16[400,256]{1,0:T(8,128)(2,1)} async-done(((bf16[400,2048]{1,0:T(8,128)(2,1)}), bf16[400,256]{1,0:T(8,128)(2,1)}) %reduce-scatter.5.cloned.1.call-update) | async-done | bytes 204816 | tf_op jit(solution)/shard_map/reduce_scatter | solution.py:43
  (68 shorter events, 13.3 us)
Async XLA Ops:
  7.2 249.3 %copy-start = (bf16[400,2048]{1,0:T(8,128)(2,1)S(1)}, bf16[400,2048]{1,0:T(8,128)(2,1)}, u32[]{:S(2)}) copy-start(bf16[400,2048]{1,0:T(8,128)(2,1)} %param.6) | copy-start | bytes 4915204
  7.2 26.7 %copy-start.1 = (bf16[32,896]{1,0:T(8,128)(2,1)S(1)}, bf16[32,896]{1,0:T(8,128)(2,1)}, u32[]{:S(2)}) copy-start(bf16[32,896]{1,0:T(8,128)(2,1)} %param.9) | copy-start | bytes 172036
  34.4 1.9 copy-start.2
  36.4 19.8 %copy-start.4 = (s32[1,64]{1,0:T(1,128)S(1)}, s32[1,64]{1,0:T(1,128)}, u32[]{:S(2)}) copy-start(s32[1,64]{1,0:T(1,128)} %param.11) | copy-start | bytes 772
  36.4 20.5 %copy-start.5 = (s32[1,64]{1,0:T(1,128)S(1)}, s32[1,64]{1,0:T(1,128)}, u32[]{:S(2)}) copy-start(s32[1,64]{1,0:T(1,128)} %param.10) | copy-start | bytes 772
  36.4 225.2 %all-to-all-start = ((bf16[64,32,896]{2,1,0:T(8,128)(2,1)}), bf16[64,32,896]{2,1,0:T(8,128)(2,1)}, u32[]{:S(2)}, u32[]{:S(2)}) async-start(bf16[64,32,896]{2,1,0:T(8,128)(2,1)} %bitcast.24), calls=%async_computation | async-start | bytes 7340032 | tf_op jit(solution)/shard_map/all_to_all | solution.py:11
  55.4 201.1 %all-gather.2.cloned.1.call-start = ((), (), s32[]{:S(2)}) async-start(), calls=%async_computation.3 | async-start | bytes 3727360 | tf_op jit(solution)/shard_map/all_gather | solution.py:52
  56.1 915.3 %reduce-scatter.7.cloned.1.call-start = ((), (), s32[]{:S(2)}) async-start(), calls=%async_computation.5 | async-start | bytes 3727360
  58.8 202.8 %copy-start.3 = (bf16[400,896]{1,0:T(8,128)(2,1)S(1)}, bf16[400,896]{1,0:T(8,128)(2,1)}, u32[]{:S(2)}) copy-start(bf16[400,896]{1,0:T(8,128)(2,1)} %param.7) | copy-start | bytes 2150404
  276.3 737.4 %reduce-scatter.5.cloned.1.call-start = ((), (), s32[]{:S(2)}) async-start(), calls=%async_computation.4 | async-start | bytes 1843200 | tf_op jit(solution)/shard_map/reduce_scatter | solution.py:43
  276.3 4.1 copy-start.6
Sparse Core Ops, SparseCore 0:
  59.2 197.2 all-gather.1
  276.4 695.0 reduce-scatter.6
  975.1 38.4 reduce-scatter.4
